TPU v7x, 256 devices: a whole 4x4x8 slice. The times are simulated.
256 devices in a mesh: row: 16 (over z, core), col: 16 (over y, x).
Axes of the slice: x: 4, y: 4, z: 8, core: 2. Of those that a mesh axis runs over, the one named last changes fastest.
Arguments:
- right_sides: float32 [4, 1024, 4096], P(None, 'row', 'col'), may hold values from -6 to 6
- low_left: bfloat16 [6, 4096, 128], P(None, 'col'), may hold values from -0.25 to 0.25
- low_right: bfloat16 [6, 4096, 128], P(None, 'col'), may hold values from -0.09375 to 0.09375
- up_left: bfloat16 [6, 4096, 128], P(None, 'col'), may hold values from -0.25 to 0.25
- up_right: bfloat16 [6, 4096, 128], P(None, 'col'), may hold values from -0.09375 to 0.09375
- low_ranks: int32 [6], replicated, may hold values from 1 to 4
- up_ranks: int32 [6], replicated, may hold values from 1 to 4
- inv_lower: bfloat16 [4, 4096, 4096], P(None, 'col', 'row'), may hold values from -0.09375 to 0.09375
- inv_upper: bfloat16 [4, 4096, 4096], P(None, 'col', 'row'), may hold values from -0.09375 to 0.09375
Outputs:
- solution: float32 [4, 1024, 4096], P(None, 'row', 'col')
Inputs may be any that keep to these rules, and one draw needn't show every extreme that they name: `low_ranks`: factor columns beyond 32 times this value are padding with arbitrary values and must be masked out. `up_ranks`: factor columns beyond 32 times this value are padding with arbitrary values and must be masked out.
All inputs are finite; a program needn't handle non-finite values.
Results may differ from a plain program's by a relative error of at most 0.03.
Values may be sent and summed in bfloat16 or wider, within the bound.
No kernel may reach another device: no remote copies, remote signals or barrier semaphores. Data moves between devices by JAX's collectives and lax.ppermute only.
A program may use at most 64 MiB of HBM per device.

v0:
```python
import jax
import jax.numpy as jnp
import numpy as np
from jax import lax
from jax.sharding import PartitionSpec as P

RBLK = 32


def laid_out(parts, dim):
    parts = jnp.moveaxis(parts, 0, dim)
    lengths = parts.shape
    return parts.reshape(*lengths[:dim], lengths[dim] * lengths[dim + 1], *lengths[dim + 2 :])


def from_everyone(value, axis):
    length = lax.axis_size(axis)
    return lax.all_to_all(
        jnp.broadcast_to(value[None], (length, *value.shape)), axis, 0, 0, tiled=True
    )


def gathered_copies(value, axis, dim):
    return laid_out(from_everyone(value, axis), dim)


def of_everyone(value, axis):
    everything = from_everyone(value, axis)
    return jnp.sum(everything.astype(jnp.float32), axis=0)


def rank_mask(ranks, pair_index, rank_cols):
    columns = jnp.arange(rank_cols, dtype=jnp.int32)
    return (columns[None, :] < RBLK * ranks[pair_index][:, None]).astype(jnp.float32)


def times_inverse(block, inverse):
    return lax.dot_general(
        block, inverse, (((1,), (1,)), ((), ())), preferred_element_type=jnp.float32
    )


def fold_columns(whole, piece):
    return times_inverse(whole, piece)


def shards(
    right_sides, low_left, low_right, up_left, up_right, low_ranks, up_ranks, inv_lower, inv_upper
):
    tile_count = right_sides.shape[0]
    rank_cols = low_left.shape[2]
    residual = right_sides
    forward = []
    for section in range(tile_count):
        rounded = residual[section].astype(jnp.bfloat16)
        whole = gathered_copies(rounded, "col", 1)
        solved = fold_columns(whole, lax.all_gather(inv_lower[section], "row", axis=1, tiled=True))
        forward.append(solved)
        if section + 1 < tile_count:
            pair_index = np.array(
                [tile * (tile - 1) // 2 + section for tile in range(section + 1, tile_count)],
                dtype=np.int32,
            )
            projections = jnp.einsum(
                "nw,mwr->mnr",
                solved.astype(jnp.bfloat16),
                low_right[pair_index],
                preferred_element_type=jnp.float32,
            )
            summed = of_everyone(projections.astype(jnp.bfloat16), "col").astype(jnp.float32)
            masked = (summed * rank_mask(low_ranks, pair_index, rank_cols)[:, None, :]).astype(
                jnp.bfloat16
            )
            update = jnp.einsum(
                "mnr,mwr->mnw", masked, low_left[pair_index], preferred_element_type=jnp.float32
            )
            residual = residual.at[section + 1 :].add(-update)
    state = jnp.stack(forward)
    solutions = [None] * tile_count
    for section in range(tile_count - 1, -1, -1):
        rounded = state[section].astype(jnp.bfloat16)
        whole = gathered_copies(rounded, "col", 1)
        solved = fold_columns(whole, lax.all_gather(inv_upper[section], "row", axis=1, tiled=True))
        solutions[section] = solved
        if section > 0:
            pair_index = np.array(
                [section * (section - 1) // 2 + tile for tile in range(section)], dtype=np.int32
            )
            projections = jnp.einsum(
                "nw,mwr->mnr",
                solved.astype(jnp.bfloat16),
                up_right[pair_index],
                preferred_element_type=jnp.float32,
            )
            summed = of_everyone(projections.astype(jnp.bfloat16), "col").astype(jnp.float32)
            masked = (summed * rank_mask(up_ranks, pair_index, rank_cols)[:, None, :]).astype(
                jnp.bfloat16
            )
            update = jnp.einsum(
                "mnr,mwr->mnw", masked, up_left[pair_index], preferred_element_type=jnp.float32
            )
            state = state.at[:section].add(-update)
    return jnp.stack(solutions)


def solution(mesh):
    in_specs = (
        P(None, "row", "col"),
        P(None, "col", None),
        P(None, "col", None),
        P(None, "col", None),
        P(None, "col", None),
        P(),
        P(),
        P(None, "col", "row"),
        P(None, "col", "row"),
    )
    out_specs = P(None, "row", "col")
    return jax.shard_map(shards, mesh=mesh, in_specs=in_specs, out_specs=out_specs, check_vma=False)
```

profile of v0, /device:TPU:1, one launch (start us, length us, event | category | flops | bytes accessed | tf_op | source)
XLA Modules:
  0.0 357.1 jit_solution(16431836217036689485)
XLA Ops:
  13.4 7.6 %all-to-all-start = ((bf16[16,64,256]{2,1,0:T(8,128)(2,1)}), bf16[16,64,256]{2,1,0:T(8,128)(2,1)S(1)}, u32[]{:S(2)}, u32[]{:S(2)}) async-start(bf16[16,64,256]{2,1,0:T(8,128)(2,1)} %broadcast_in_dim.83), calls=%async_computation | async-start | bytes 1048576 | tf_op jit(solution)/shard_map/all_to_all | solution.py:18
  21.6 9.9 %all-to-all-done = bf16[16,64,256]{2,1,0:T(8,128)(2,1)S(1)} async-done(((bf16[16,64,256]{2,1,0:T(8,128)(2,1)}), bf16[16,64,256]{2,1,0:T(8,128)(2,1)S(1)}, u32[]{:S(2)}, u32[]{:S(2)}) %all-to-all-start) | async-done | bytes 524320 | tf_op jit(solution)/shard_map/all_to_all | solution.py:18
  31.6 22.7 %all-gather.17.cloned.1.call-done = bf16[1,256,4096]{2,1,0:T(8,128)(2,1)} async-done(((bf16[1,256,256]{2,1,0:T(8,128)(2,1)}), bf16[1,256,4096]{2,1,0:T(8,128)(2,1)}) %all-gather.17.cloned.1.call-update) | async-done | bytes 2097168 | tf_op jit(solution)/shard_map/all_gather | solution.py:57
  57.9 6.5 %all-to-all-start.1 = ((bf16[16,3,64,128]{3,2,1,0:T(8,128)(2,1)}), bf16[16,3,64,128]{3,2,1,0:T(8,128)(2,1)S(1)}, u32[]{:S(2)}, u32[]{:S(2)}) async-start(bf16[16,3,64,128]{3,2,1,0:T(8,128)(2,1)} %broadcast_in_dim.85), calls=%async_computation.1 | async-start | bytes 1572864 | tf_op jit(solution)/shard_map/all_to_all | solution.py:18
  66.4 11.7 %all-to-all-done.1 = bf16[16,3,64,128]{3,2,1,0:T(8,128)(2,1)S(1)} async-done(((bf16[16,3,64,128]{3,2,1,0:T(8,128)(2,1)}), bf16[16,3,64,128]{3,2,1,0:T(8,128)(2,1)S(1)}, u32[]{:S(2)}, u32[]{:S(2)}) %all-to-all-start.1) | async-done | bytes 786464 | tf_op jit(solution)/shard_map/all_to_all | solution.py:18
  79.3 3.6 %all-to-all-start.2 = ((bf16[16,64,256]{2,1,0:T(8,128)(2,1)}), bf16[16,64,256]{2,1,0:T(8,128)(2,1)S(1)}, u32[]{:S(2)}, u32[]{:S(2)}) async-start(bf16[16,64,256]{2,1,0:T(8,128)(2,1)} %broadcast_in_dim.89), calls=%async_computation.2 | async-start | bytes 1048576 | tf_op jit(solution)/shard_map/all_to_all | solution.py:18
  83.5 9.5 %all-to-all-done.2 = bf16[16,64,256]{2,1,0:T(8,128)(2,1)S(1)} async-done(((bf16[16,64,256]{2,1,0:T(8,128)(2,1)}), bf16[16,64,256]{2,1,0:T(8,128)(2,1)S(1)}, u32[]{:S(2)}, u32[]{:S(2)}) %all-to-all-start.2) | async-done | bytes 524320 | tf_op jit(solution)/shard_map/all_to_all | solution.py:18
  93.1 3.1 all-gather.19.cloned.1.call-done
  99.7 6.5 %all-to-all-start.3 = ((bf16[16,2,64,128]{3,2,1,0:T(8,128)(2,1)}), bf16[16,2,64,128]{3,2,1,0:T(8,128)(2,1)S(1)}, u32[]{:S(2)}, u32[]{:S(2)}) async-start(bf16[16,2,64,128]{3,2,1,0:T(8,128)(2,1)} %broadcast_in_dim.91), calls=%async_computation.3 | async-start | bytes 1048576 | tf_op jit(solution)/shard_map/all_to_all | solution.py:18
  107.5 9.5 %all-to-all-done.3 = bf16[16,2,64,128]{3,2,1,0:T(8,128)(2,1)S(1)} async-done(((bf16[16,2,64,128]{3,2,1,0:T(8,128)(2,1)}), bf16[16,2,64,128]{3,2,1,0:T(8,128)(2,1)S(1)}, u32[]{:S(2)}, u32[]{:S(2)}) %all-to-all-start.3) | async-done | bytes 524320 | tf_op jit(solution)/shard_map/all_to_all | solution.py:18
  118.1 3.6 %all-to-all-start.4 = ((bf16[16,64,256]{2,1,0:T(8,128)(2,1)}), bf16[16,64,256]{2,1,0:T(8,128)(2,1)S(1)}, u32[]{:S(2)}, u32[]{:S(2)}) async-start(bf16[16,64,256]{2,1,0:T(8,128)(2,1)} %broadcast_in_dim.187), calls=%async_computation.4 | async-start | bytes 1048576 | tf_op jit(solution)/shard_map/all_to_all | solution.py:18
  122.4 9.3 %all-to-all-done.4 = bf16[16,64,256]{2,1,0:T(8,128)(2,1)S(1)} async-done(((bf16[16,64,256]{2,1,0:T(8,128)(2,1)}), bf16[16,64,256]{2,1,0:T(8,128)(2,1)S(1)}, u32[]{:S(2)}, u32[]{:S(2)}) %all-to-all-start.4) | async-done | bytes 524320 | tf_op jit(solution)/shard_map/all_to_all | solution.py:18
  131.8 6.3 %all-gather.21.cloned.1.call-done = bf16[1,256,4096]{2,1,0:T(8,128)(2,1)} async-done(((bf16[1,256,256]{2,1,0:T(8,128)(2,1)}), bf16[1,256,4096]{2,1,0:T(8,128)(2,1)}) %all-gather.21.cloned.1.call-update) | async-done | bytes 2097168 | tf_op jit(solution)/shard_map/all_gather | solution.py:57
  141.3 6.5 %all-to-all-start.5 = ((bf16[16,1,64,128]{3,2,1,0:T(8,128)(2,1)}), bf16[16,1,64,128]{3,2,1,0:T(8,128)(2,1)S(1)}, u32[]{:S(2)}, u32[]{:S(2)}) async-start(bf16[16,1,64,128]{3,2,1,0:T(8,128)(2,1)} %broadcast_in_dim.191), calls=%async_computation.5 | async-start | bytes 524288 | tf_op jit(solution)/shard_map/all_to_all | solution.py:18
  149.0 7.1 %all-to-all-done.5 = bf16[16,1,64,128]{3,2,1,0:T(8,128)(2,1)S(1)} async-done(((bf16[16,1,64,128]{3,2,1,0:T(8,128)(2,1)}), bf16[16,1,64,128]{3,2,1,0:T(8,128)(2,1)S(1)}, u32[]{:S(2)}, u32[]{:S(2)}) %all-to-all-start.5) | async-done | bytes 262176 | tf_op jit(solution)/shard_map/all_to_all | solution.py:18
  156.3 12.8 %all_to_all.70 = bf16[16,64,256]{2,1,0:T(8,128)(2,1)S(1)} all-to-all(bf16[16,64,256]{2,1,0:T(8,128)(2,1)S(1)} %broadcast_in_dim.195), channel_id=1, replica_groups=mesh['row'=16,'col'=16] {'col'}, dimensions={0} | all-to-all | bytes 1048576 | tf_op jit(solution)/shard_map/all_to_all | solution.py:18
  169.2 10.6 %all-gather.23.cloned.1.call-done = bf16[1,256,4096]{2,1,0:T(8,128)(2,1)} async-done(((bf16[1,256,256]{2,1,0:T(8,128)(2,1)}), bf16[1,256,4096]{2,1,0:T(8,128)(2,1)}) %all-gather.23.cloned.1.call-update) | async-done | bytes 2097168 | tf_op jit(solution)/shard_map/all_gather | solution.py:57
  183.1 6.5 %all-to-all-start.7 = ((bf16[16,64,256]{2,1,0:T(8,128)(2,1)}), bf16[16,64,256]{2,1,0:T(8,128)(2,1)S(1)}, u32[]{:S(2)}, u32[]{:S(2)}) async-start(bf16[16,64,256]{2,1,0:T(8,128)(2,1)} %broadcast_in_dim.196), calls=%async_computation.7 | async-start | bytes 1048576 | tf_op jit(solution)/shard_map/all_to_all | solution.py:18
  190.2 10.2 %all-to-all-done.7 = bf16[16,64,256]{2,1,0:T(8,128)(2,1)S(1)} async-done(((bf16[16,64,256]{2,1,0:T(8,128)(2,1)}), bf16[16,64,256]{2,1,0:T(8,128)(2,1)S(1)}, u32[]{:S(2)}, u32[]{:S(2)}) %all-to-all-start.7) | async-done | bytes 524320 | tf_op jit(solution)/shard_map/all_to_all | solution.py:18
  200.5 21.2 %all-gather.25.cloned.1.call-done = bf16[1,256,4096]{2,1,0:T(8,128)(2,1)} async-done(((bf16[1,256,256]{2,1,0:T(8,128)(2,1)}), bf16[1,256,4096]{2,1,0:T(8,128)(2,1)}) %all-gather.25.cloned.1.call-update) | async-done | bytes 2097168 | tf_op jit(solution)/shard_map/all_gather | solution.py:83
  225.3 6.5 %all-to-all-start.8 = ((bf16[16,3,64,128]{3,2,1,0:T(8,128)(2,1)}), bf16[16,3,64,128]{3,2,1,0:T(8,128)(2,1)S(1)}, u32[]{:S(2)}, u32[]{:S(2)}) async-start(bf16[16,3,64,128]{3,2,1,0:T(8,128)(2,1)} %broadcast_in_dim.197), calls=%async_computation.8 | async-start | bytes 1572864 | tf_op jit(solution)/shard_map/all_to_all | solution.py:18
  233.2 12.3 %all-to-all-done.8 = bf16[16,3,64,128]{3,2,1,0:T(8,128)(2,1)S(1)} async-done(((bf16[16,3,64,128]{3,2,1,0:T(8,128)(2,1)}), bf16[16,3,64,128]{3,2,1,0:T(8,128)(2,1)S(1)}, u32[]{:S(2)}, u32[]{:S(2)}) %all-to-all-start.8) | async-done | bytes 786464 | tf_op jit(solution)/shard_map/all_to_all | solution.py:18
  246.6 3.6 %all-to-all-start.9 = ((bf16[16,64,256]{2,1,0:T(8,128)(2,1)}), bf16[16,64,256]{2,1,0:T(8,128)(2,1)S(1)}, u32[]{:S(2)}, u32[]{:S(2)}) async-start(bf16[16,64,256]{2,1,0:T(8,128)(2,1)} %broadcast_in_dim.202), calls=%async_computation.9 | async-start | bytes 1048576 | tf_op jit(solution)/shard_map/all_to_all | solution.py:18
  251.6 8.8 %all-to-all-done.9 = bf16[16,64,256]{2,1,0:T(8,128)(2,1)S(1)} async-done(((bf16[16,64,256]{2,1,0:T(8,128)(2,1)}), bf16[16,64,256]{2,1,0:T(8,128)(2,1)S(1)}, u32[]{:S(2)}, u32[]{:S(2)}) %all-to-all-start.9) | async-done | bytes 524320 | tf_op jit(solution)/shard_map/all_to_all | solution.py:18
  266.8 6.5 %all-to-all-start.10 = ((bf16[16,2,64,128]{3,2,1,0:T(8,128)(2,1)}), bf16[16,2,64,128]{3,2,1,0:T(8,128)(2,1)S(1)}, u32[]{:S(2)}, u32[]{:S(2)}) async-start(bf16[16,2,64,128]{3,2,1,0:T(8,128)(2,1)} %broadcast_in_dim.203), calls=%async_computation.10 | async-start | bytes 1048576 | tf_op jit(solution)/shard_map/all_to_all | solution.py:18
  274.7 9.5 %all-to-all-done.10 = bf16[16,2,64,128]{3,2,1,0:T(8,128)(2,1)S(1)} async-done(((bf16[16,2,64,128]{3,2,1,0:T(8,128)(2,1)}), bf16[16,2,64,128]{3,2,1,0:T(8,128)(2,1)S(1)}, u32[]{:S(2)}, u32[]{:S(2)}) %all-to-all-start.10) | async-done | bytes 524320 | tf_op jit(solution)/shard_map/all_to_all | solution.py:18
  284.5 13.4 %all_to_all.71 = bf16[16,64,256]{2,1,0:T(8,128)(2,1)S(1)} all-to-all(bf16[16,64,256]{2,1,0:T(8,128)(2,1)S(1)} %broadcast_in_dim.208), channel_id=1, replica_groups=mesh['row'=16,'col'=16] {'col'}, dimensions={0} | all-to-all | bytes 1048576 | tf_op jit(solution)/shard_map/all_to_all | solution.py:18
  297.9 7.4 %all-gather.29.cloned.1.call-done = bf16[1,256,4096]{2,1,0:T(8,128)(2,1)} async-done(((bf16[1,256,256]{2,1,0:T(8,128)(2,1)}), bf16[1,256,4096]{2,1,0:T(8,128)(2,1)}) %all-gather.29.cloned.1.call-update) | async-done | bytes 2097168 | tf_op jit(solution)/shard_map/all_gather | solution.py:83
  308.5 6.5 %all-to-all-start.12 = ((bf16[16,1,64,128]{3,2,1,0:T(8,128)(2,1)}), bf16[16,1,64,128]{3,2,1,0:T(8,128)(2,1)S(1)}, u32[]{:S(2)}, u32[]{:S(2)}) async-start(bf16[16,1,64,128]{3,2,1,0:T(8,128)(2,1)} %broadcast_in_dim.210), calls=%async_computation.12 | async-start | bytes 524288 | tf_op jit(solution)/shard_map/all_to_all | solution.py:18
  315.1 8.2 %all-to-all-done.12 = bf16[16,1,64,128]{3,2,1,0:T(8,128)(2,1)S(1)} async-done(((bf16[16,1,64,128]{3,2,1,0:T(8,128)(2,1)}), bf16[16,1,64,128]{3,2,1,0:T(8,128)(2,1)S(1)}, u32[]{:S(2)}, u32[]{:S(2)}) %all-to-all-start.12) | async-done | bytes 262176 | tf_op jit(solution)/shard_map/all_to_all | solution.py:18
  323.5 12.8 %all_to_all.72 = bf16[16,64,256]{2,1,0:T(8,128)(2,1)S(1)} all-to-all(bf16[16,64,256]{2,1,0:T(8,128)(2,1)S(1)} %broadcast_in_dim.214), channel_id=1, replica_groups=mesh['row'=16,'col'=16] {'col'}, dimensions={0} | all-to-all | bytes 1048576 | tf_op jit(solution)/shard_map/all_to_all | solution.py:18
  336.4 10.8 %all-gather.31.cloned.1.call-done = bf16[1,256,4096]{2,1,0:T(8,128)(2,1)} async-done(((bf16[1,256,256]{2,1,0:T(8,128)(2,1)}), bf16[1,256,4096]{2,1,0:T(8,128)(2,1)}) %all-gather.31.cloned.1.call-update) | async-done | bytes 2097168 | tf_op jit(solution)/shard_map/all_gather | solution.py:83
  (122 shorter events, 51.3 us)
Async XLA Ops:
  6.5 14.5 %copy-start.10 = (s32[3]{0:T(128)S(1)}, s32[3]{0:T(128)}, u32[]{:S(2)}) copy-start(s32[3]{0:T(128)} %constant.313) | copy-start | bytes 40
  6.5 6.0 %copy-start.6 = (f32[4,64,256]{2,1,0:T(8,128)S(1)}, f32[4,64,256]{2,1,0:T(8,128)}, u32[]{:S(2)}) copy-start(f32[4,64,256]{2,1,0:T(8,128)} %param.45) | copy-start | bytes 786436
  6.5 14.5 %copy-start.2 = (bf16[6,256,128]{2,1,0:T(8,128)(2,1)S(1)}, bf16[6,256,128]{2,1,0:T(8,128)(2,1)}, u32[]{:S(2)}) copy-start(bf16[6,256,128]{2,1,0:T(8,128)(2,1)} %param.47) | copy-start | bytes 1179652
  6.5 47.7 %all-gather.17.cloned.1.call-start = ((), (), s32[]{:S(2)}) async-start(), calls=%async_computation.14 | async-start | bytes 2228224 | tf_op jit(solution)/shard_map/all_gather | solution.py:57
  8.5 87.7 %all-gather.19.cloned.1.call-start = ((), (), s32[]{:S(2)}) async-start(), calls=%async_computation.15 | async-start | bytes 2228224 | tf_op jit(solution)/shard_map/all_gather | solution.py:57
  9.3 128.8 %all-gather.21.cloned.1.call-start = ((), (), s32[]{:S(2)}) async-start(), calls=%async_computation.16 | async-start | bytes 2228224 | tf_op jit(solution)/shard_map/all_gather | solution.py:57
  10.0 169.8 %all-gather.23.cloned.1.call-start = ((), (), s32[]{:S(2)}) async-start(), calls=%async_computation.17 | async-start | bytes 2228224 | tf_op jit(solution)/shard_map/all_gather | solution.py:57
  10.6 211.0 %all-gather.25.cloned.1.call-start = ((), (), s32[]{:S(2)}) async-start(), calls=%async_computation.18 | async-start | bytes 2228224 | tf_op jit(solution)/shard_map/all_gather | solution.py:83
  13.4 18.1 %all-to-all-start = ((bf16[16,64,256]{2,1,0:T(8,128)(2,1)}), bf16[16,64,256]{2,1,0:T(8,128)(2,1)S(1)}, u32[]{:S(2)}, u32[]{:S(2)}) async-start(bf16[16,64,256]{2,1,0:T(8,128)(2,1)} %broadcast_in_dim.83), calls=%async_computation | async-start | bytes 1048576 | tf_op jit(solution)/shard_map/all_to_all | solution.py:18
  56.6 8.4 %copy-start.3 = (bf16[6,256,128]{2,1,0:T(8,128)(2,1)S(1)}, bf16[6,256,128]{2,1,0:T(8,128)(2,1)}, u32[]{:S(2)}) copy-start(bf16[6,256,128]{2,1,0:T(8,128)(2,1)} %param.46) | copy-start | bytes 1179652
  56.6 9.0 %copy-start = (s32[6]{0:T(128)S(1)}, s32[6]{0:T(128)}, u32[]{:S(2)}) copy-start(s32[6]{0:T(128)} %param.50) | copy-start | bytes 76
  57.9 20.2 %all-to-all-start.1 = ((bf16[16,3,64,128]{3,2,1,0:T(8,128)(2,1)}), bf16[16,3,64,128]{3,2,1,0:T(8,128)(2,1)S(1)}, u32[]{:S(2)}, u32[]{:S(2)}) async-start(bf16[16,3,64,128]{3,2,1,0:T(8,128)(2,1)} %broadcast_in_dim.85), calls=%async_computation.1 | async-start | bytes 1572864 | tf_op jit(solution)/shard_map/all_to_all | solution.py:18
  64.4 198.9 %all-gather.27.cloned.1.call-start = ((), (), s32[]{:S(2)}) async-start(), calls=%async_computation.19 | async-start | bytes 2228224 | tf_op jit(solution)/shard_map/all_gather | solution.py:83
  65.0 17.9 %copy-start.9 = (s32[2]{0:T(128)S(1)}, s32[2]{0:T(128)}, u32[]{:S(2)}) copy-start(s32[2]{0:T(128)} %constant.316) | copy-start | bytes 28
  79.3 13.8 %all-to-all-start.2 = ((bf16[16,64,256]{2,1,0:T(8,128)(2,1)}), bf16[16,64,256]{2,1,0:T(8,128)(2,1)S(1)}, u32[]{:S(2)}, u32[]{:S(2)}) async-start(bf16[16,64,256]{2,1,0:T(8,128)(2,1)} %broadcast_in_dim.89), calls=%async_computation.2 | async-start | bytes 1048576 | tf_op jit(solution)/shard_map/all_to_all | solution.py:18
  99.7 17.4 %all-to-all-start.3 = ((bf16[16,2,64,128]{3,2,1,0:T(8,128)(2,1)}), bf16[16,2,64,128]{3,2,1,0:T(8,128)(2,1)S(1)}, u32[]{:S(2)}, u32[]{:S(2)}) async-start(bf16[16,2,64,128]{3,2,1,0:T(8,128)(2,1)} %broadcast_in_dim.91), calls=%async_computation.3 | async-start | bytes 1048576 | tf_op jit(solution)/shard_map/all_to_all | solution.py:18
  118.1 13.6 %all-to-all-start.4 = ((bf16[16,64,256]{2,1,0:T(8,128)(2,1)}), bf16[16,64,256]{2,1,0:T(8,128)(2,1)S(1)}, u32[]{:S(2)}, u32[]{:S(2)}) async-start(bf16[16,64,256]{2,1,0:T(8,128)(2,1)} %broadcast_in_dim.187), calls=%async_computation.4 | async-start | bytes 1048576 | tf_op jit(solution)/shard_map/all_to_all | solution.py:18
  121.7 183.6 %all-gather.29.cloned.1.call-start = ((), (), s32[]{:S(2)}) async-start(), calls=%async_computation.20 | async-start | bytes 2228224 | tf_op jit(solution)/shard_map/all_gather | solution.py:83
  141.3 14.8 %all-to-all-start.5 = ((bf16[16,1,64,128]{3,2,1,0:T(8,128)(2,1)}), bf16[16,1,64,128]{3,2,1,0:T(8,128)(2,1)S(1)}, u32[]{:S(2)}, u32[]{:S(2)}) async-start(bf16[16,1,64,128]{3,2,1,0:T(8,128)(2,1)} %broadcast_in_dim.191), calls=%async_computation.5 | async-start | bytes 524288 | tf_op jit(solution)/shard_map/all_to_all | solution.py:18
  179.8 9.8 %copy-start.8 = (s32[3]{0:T(128)S(1)}, s32[3]{0:T(128)}, u32[]{:S(2)}) copy-start(s32[3]{0:T(128)} %constant.319) | copy-start | bytes 40
  179.8 9.8 %copy-start.4 = (bf16[6,256,128]{2,1,0:T(8,128)(2,1)S(1)}, bf16[6,256,128]{2,1,0:T(8,128)(2,1)}, u32[]{:S(2)}) copy-start(bf16[6,256,128]{2,1,0:T(8,128)(2,1)} %param.49) | copy-start | bytes 1179652
  183.1 17.4 %all-to-all-start.7 = ((bf16[16,64,256]{2,1,0:T(8,128)(2,1)}), bf16[16,64,256]{2,1,0:T(8,128)(2,1)S(1)}, u32[]{:S(2)}, u32[]{:S(2)}) async-start(bf16[16,64,256]{2,1,0:T(8,128)(2,1)} %broadcast_in_dim.196), calls=%async_computation.7 | async-start | bytes 1048576 | tf_op jit(solution)/shard_map/all_to_all | solution.py:18
  221.6 10.2 %copy-start.5 = (bf16[6,256,128]{2,1,0:T(8,128)(2,1)S(1)}, bf16[6,256,128]{2,1,0:T(8,128)(2,1)}, u32[]{:S(2)}) copy-start(bf16[6,256,128]{2,1,0:T(8,128)(2,1)} %param.48) | copy-start | bytes 1179652
  224.0 8.4 %copy-start.1 = (s32[6]{0:T(128)S(1)}, s32[6]{0:T(128)}, u32[]{:S(2)}) copy-start(s32[6]{0:T(128)} %param.51) | copy-start | bytes 76
  225.3 20.2 %all-to-all-start.8 = ((bf16[16,3,64,128]{3,2,1,0:T(8,128)(2,1)}), bf16[16,3,64,128]{3,2,1,0:T(8,128)(2,1)S(1)}, u32[]{:S(2)}, u32[]{:S(2)}) async-start(bf16[16,3,64,128]{3,2,1,0:T(8,128)(2,1)} %broadcast_in_dim.197), calls=%async_computation.8 | async-start | bytes 1572864 | tf_op jit(solution)/shard_map/all_to_all | solution.py:18
  231.8 19.2 %copy-start.7 = (s32[2]{0:T(128)S(1)}, s32[2]{0:T(128)}, u32[]{:S(2)}) copy-start(s32[2]{0:T(128)} %constant.322) | copy-start | bytes 28
  246.6 13.8 %all-to-all-start.9 = ((bf16[16,64,256]{2,1,0:T(8,128)(2,1)}), bf16[16,64,256]{2,1,0:T(8,128)(2,1)S(1)}, u32[]{:S(2)}, u32[]{:S(2)}) async-start(bf16[16,64,256]{2,1,0:T(8,128)(2,1)} %broadcast_in_dim.202), calls=%async_computation.9 | async-start | bytes 1048576 | tf_op jit(solution)/shard_map/all_to_all | solution.py:18
  250.3 96.9 %all-gather.31.cloned.1.call-start = ((), (), s32[]{:S(2)}) async-start(), calls=%async_computation.21 | async-start | bytes 2228224 | tf_op jit(solution)/shard_map/all_gather | solution.py:83
  266.8 17.4 %all-to-all-start.10 = ((bf16[16,2,64,128]{3,2,1,0:T(8,128)(2,1)}), bf16[16,2,64,128]{3,2,1,0:T(8,128)(2,1)S(1)}, u32[]{:S(2)}, u32[]{:S(2)}) async-start(bf16[16,2,64,128]{3,2,1,0:T(8,128)(2,1)} %broadcast_in_dim.203), calls=%async_computation.10 | async-start | bytes 1048576 | tf_op jit(solution)/shard_map/all_to_all | solution.py:18
  308.5 14.7 %all-to-all-start.12 = ((bf16[16,1,64,128]{3,2,1,0:T(8,128)(2,1)}), bf16[16,1,64,128]{3,2,1,0:T(8,128)(2,1)S(1)}, u32[]{:S(2)}, u32[]{:S(2)}) async-start(bf16[16,1,64,128]{3,2,1,0:T(8,128)(2,1)} %broadcast_in_dim.210), calls=%async_computation.12 | async-start | bytes 524288 | tf_op jit(solution)/shard_map/all_to_all | solution.py:18
Sparse Core Ops, SparseCore 0:
  9.1 45.1 all-gather.16
  56.0 40.1 all-gather.18
  98.0 40.0 all-gather.20
  139.7 40.0 all-gather.22
  181.4 40.1 all-gather.24
  223.2 40.1 all-gather.26
  265.1 40.0 all-gather.28
  307.0 40.0 all-gather.30
where the time goes:
time: 359 us; the launch traced here: 357 us
  waiting for transfers between devices  195 us (54%)
  starting transfers between devices  64.4 us (18%)
  blocking collectives  39 us (11%)
  local copies, waits for them, and re-layouts  21.9 us (6%)
  matrix products  20.8 us (6%)
  between operations  14.5 us (4%)
    all_to_all x11, waiting for transfers between devices, from_everyone(): lax.all_to_all(jnp.broadcast_to(value[None], (length, *value.shape)), axi...  106 us
    all_to_all x11, starting transfers between devices, from_everyone(): lax.all_to_all(jnp.broadcast_to(value[None], (length, *value.shape)), axi...  64.1 us
    all_gather x4, waiting for transfers between devices, shards(): lax.all_gather(inv_lower[section], 'row', axis=1, tiled=True)  42.8 us
    all_gather x4, waiting for transfers between devices, shards(): lax.all_gather(inv_upper[section], 'row', axis=1, tiled=True)  42.2 us
    all_to_all x3, blocking collectives, from_everyone(): lax.all_to_all(jnp.broadcast_to(value[None], (length, *value.shape)), axi...  39 us
    dot_general x8, matrix products, times_inverse(): lax.dot_general(block, inverse, (((1,), (1,)), ((), ())), preferred_eleme...  18.9 us
    broadcast_in_dim x19, local copies, waits for them, and re-layouts, from_everyone(): jnp.broadcast_to(value[None], (length, *value.shape))  9.98 us
  transfers between devices with their start and end apart: 19, of which 19 were waited for; matrix products, arithmetic and copies ran while one was open for 11% of the time, Pallas kernels for 0%

commit v1 on v0

--- a/solution.py
+++ b/solution.py
@@ -54,7 +54,13 @@
     for section in range(tile_count):
         rounded = residual[section].astype(jnp.bfloat16)
         whole = gathered_copies(rounded, "col", 1)
-        solved = fold_columns(whole, lax.all_gather(inv_lower[section], "row", axis=1, tiled=True))
+        solved = fold_columns(
+            whole,
+            jnp.concatenate(
+                lax.all_to_all(jnp.stack([inv_lower[section]] * lax.axis_size("row")), "row", 0, 0),
+                axis=1,
+            ),
+        )
         forward.append(solved)
         if section + 1 < tile_count:
             pair_index = np.array(

time: 359 us -> 480 us (1.34); the launches traced: 357 us -> 470 us
  waiting for transfers between devices: 195 us -> 263 us
  blocking collectives: 39 us -> 78.6 us
  local copies, waits for them, and re-layouts: 21.9 us -> 29.7 us
    all_to_all x0 -> x4, waiting for transfers between devices: none -> 191 us  [shards(): lax.all_to_all(jnp.stack([inv_lower[section]] * lax.axis_size('row')), 'r...]
    all_gather x4 -> x0, waiting for transfers between devices: 42.8 us -> none  [shards(): lax.all_gather(inv_lower[section], 'row', axis=1, tiled=True)]
    all_gather x4, waiting for transfers between devices: 42.2 us -> 0.08 us  [shards(): lax.all_gather(inv_upper[section], 'row', axis=1, tiled=True)]
    all_to_all x3 -> x6, blocking collectives: 39 us -> 78.6 us  [from_everyone(): lax.all_to_all(jnp.broadcast_to(value[None], (length, *value.shape)), axi...]
    all_to_all x11 -> x8, waiting for transfers between devices: 106 us -> 70.5 us  [from_everyone(): lax.all_to_all(jnp.broadcast_to(value[None], (length, *value.shape)), axi...]
    all_to_all x0 -> x4, starting transfers between devices: none -> 33.5 us  [shards(): lax.all_to_all(jnp.stack([inv_lower[section]] * lax.axis_size('row')), 'r...]
    all_to_all x11 -> x8, starting transfers between devices: 64.1 us -> 32.6 us  [from_everyone(): lax.all_to_all(jnp.broadcast_to(value[None], (length, *value.shape)), axi...]
    dot_general x8, matrix products: 18.9 us -> 12.5 us  [times_inverse(): lax.dot_general(block, inverse, (((1,), (1,)), ((), ())), preferred_eleme...]
  transfers between devices with their start and end apart: 19 -> 16, of which waited for: 19 -> 12; matrix products, arithmetic and copies ran while one was open for 11% -> 8% of each run, Pallas kernels for 0% -> 0%
where the time goes in v1:
time: 480 us; the launch traced here: 470 us
  waiting for transfers between devices  263 us (55%)
  blocking collectives  78.6 us (16%)
  starting transfers between devices  66.2 us (14%)
  local copies, waits for them, and re-layouts  29.7 us (6%)
  matrix products  17 us (4%)
  between operations  14.3 us (3%)
    all_to_all x4, waiting for transfers between devices, shards(): lax.all_to_all(jnp.stack([inv_lower[section]] * lax.axis_size('row')), 'r...  191 us
    all_to_all x6, blocking collectives, from_everyone(): lax.all_to_all(jnp.broadcast_to(value[None], (length, *value.shape)), axi...  78.6 us
    all_to_all x8, waiting for transfers between devices, from_everyone(): lax.all_to_all(jnp.broadcast_to(value[None], (length, *value.shape)), axi...  70.5 us
    all_to_all x4, starting transfers between devices, shards(): lax.all_to_all(jnp.stack([inv_lower[section]] * lax.axis_size('row')), 'r...  33.5 us
    all_to_all x8, starting transfers between devices, from_everyone(): lax.all_to_all(jnp.broadcast_to(value[None], (length, *value.shape)), axi...  32.6 us
    dot_general x8, matrix products, times_inverse(): lax.dot_general(block, inverse, (((1,), (1,)), ((), ())), preferred_eleme...  12.5 us
  transfers between devices with their start and end apart: 16, of which 12 were waited for; matrix products, arithmetic and copies ran while one was open for 8% of the time, Pallas kernels for 0%

profile of v1, /device:TPU:1, one launch (start us, length us, event | category | flops | bytes accessed | tf_op | source)
XLA Modules:
  0.0 470.5 jit_solution(17576627437974224374)
XLA Ops:
  8.2 7.6 %all-to-all-start = ((bf16[16,64,256]{2,1,0:T(8,128)(2,1)}), bf16[16,64,256]{2,1,0:T(8,128)(2,1)S(1)}, u32[]{:S(2)}, u32[]{:S(2)}) async-start(bf16[16,64,256]{2,1,0:T(8,128)(2,1)} %broadcast_in_dim.83), calls=%async_computation | async-start | bytes 1048576 | tf_op jit(solution)/shard_map/all_to_all | solution.py:18
  17.0 9.4 %all-to-all-done = bf16[16,64,256]{2,1,0:T(8,128)(2,1)S(1)} async-done(((bf16[16,64,256]{2,1,0:T(8,128)(2,1)}), bf16[16,64,256]{2,1,0:T(8,128)(2,1)S(1)}, u32[]{:S(2)}, u32[]{:S(2)}) %all-to-all-start) | async-done | bytes 524320 | tf_op jit(solution)/shard_map/all_to_all | solution.py:18
  27.9 10.6 %all-to-all-start.1 = ((bf16[16,256,256]{2,1,0:T(8,128)(2,1)}), bf16[16,256,256]{2,1,0:T(8,128)(2,1)S(1)}, u32[]{:S(2)}, u32[]{:S(2)}) async-start(bf16[16,256,256]{2,1,0:T(8,128)(2,1)} %stack.40), calls=%async_computation.1 | async-start | bytes 4194304 | tf_op jit(solution)/shard_map/all_to_all | solution.py:60
  40.1 47.3 %all-to-all-done.1 = bf16[16,256,256]{2,1,0:T(8,128)(2,1)S(1)} async-done(((bf16[16,256,256]{2,1,0:T(8,128)(2,1)}), bf16[16,256,256]{2,1,0:T(8,128)(2,1)S(1)}, u32[]{:S(2)}, u32[]{:S(2)}) %all-to-all-start.1) | async-done | bytes 2097184 | tf_op jit(solution)/shard_map/all_to_all | solution.py:60
  88.5 16.5 %all_to_all.90 = bf16[16,3,64,128]{3,2,1,0:T(8,128)(2,1)S(1)} all-to-all(bf16[16,3,64,128]{3,2,1,0:T(8,128)(2,1)S(1)} %broadcast_in_dim.85), channel_id=1, replica_groups=mesh['row'=16,'col'=16] {'col'}, dimensions={0} | all-to-all | bytes 1572864 | tf_op jit(solution)/shard_map/all_to_all | solution.py:18
  106.6 6.1 %all-to-all-start.4 = ((bf16[16,256,256]{2,1,0:T(8,128)(2,1)}), bf16[16,256,256]{2,1,0:T(8,128)(2,1)S(1)}, u32[]{:S(2)}, u32[]{:S(2)}) async-start(bf16[16,256,256]{2,1,0:T(8,128)(2,1)} %stack.42), calls=%async_computation.4 | async-start | bytes 4194304 | tf_op jit(solution)/shard_map/all_to_all | solution.py:60
  116.4 45.3 %all-to-all-done.4 = bf16[16,256,256]{2,1,0:T(8,128)(2,1)S(1)} async-done(((bf16[16,256,256]{2,1,0:T(8,128)(2,1)}), bf16[16,256,256]{2,1,0:T(8,128)(2,1)S(1)}, u32[]{:S(2)}, u32[]{:S(2)}) %all-to-all-start.4) | async-done | bytes 2097184 | tf_op jit(solution)/shard_map/all_to_all | solution.py:60
  162.6 3.6 all-to-all-start.3
  167.8 9.4 %all-to-all-done.3 = bf16[16,64,256]{2,1,0:T(8,128)(2,1)S(1)} async-done(((bf16[16,64,256]{2,1,0:T(8,128)(2,1)}), bf16[16,64,256]{2,1,0:T(8,128)(2,1)S(1)}, u32[]{:S(2)}, u32[]{:S(2)}) %all-to-all-start.3) | async-done | bytes 524320 | tf_op jit(solution)/shard_map/all_to_all | solution.py:18
  178.2 13.4 %all_to_all.91 = bf16[16,2,64,128]{3,2,1,0:T(8,128)(2,1)S(1)} all-to-all(bf16[16,2,64,128]{3,2,1,0:T(8,128)(2,1)S(1)} %broadcast_in_dim.91), channel_id=1, replica_groups=mesh['row'=16,'col'=16] {'col'}, dimensions={0} | all-to-all | bytes 1048576 | tf_op jit(solution)/shard_map/all_to_all | solution.py:18
  193.1 6.7 %all-to-all-start.7 = ((bf16[16,256,256]{2,1,0:T(8,128)(2,1)}), bf16[16,256,256]{2,1,0:T(8,128)(2,1)S(1)}, u32[]{:S(2)}, u32[]{:S(2)}) async-start(bf16[16,256,256]{2,1,0:T(8,128)(2,1)} %stack.44), calls=%async_computation.7 | async-start | bytes 4194304 | tf_op jit(solution)/shard_map/all_to_all | solution.py:60
  204.3 50.0 %all-to-all-done.7 = bf16[16,256,256]{2,1,0:T(8,128)(2,1)S(1)} async-done(((bf16[16,256,256]{2,1,0:T(8,128)(2,1)}), bf16[16,256,256]{2,1,0:T(8,128)(2,1)S(1)}, u32[]{:S(2)}, u32[]{:S(2)}) %all-to-all-start.7) | async-done | bytes 2097184 | tf_op jit(solution)/shard_map/all_to_all | solution.py:60
  255.1 3.6 all-to-all-start.6
  259.5 9.1 %all-to-all-done.6 = bf16[16,64,256]{2,1,0:T(8,128)(2,1)S(1)} async-done(((bf16[16,64,256]{2,1,0:T(8,128)(2,1)}), bf16[16,64,256]{2,1,0:T(8,128)(2,1)S(1)}, u32[]{:S(2)}, u32[]{:S(2)}) %all-to-all-start.6) | async-done | bytes 524320 | tf_op jit(solution)/shard_map/all_to_all | solution.py:18
  270.4 10.5 %all_to_all.92 = bf16[16,1,64,128]{3,2,1,0:T(8,128)(2,1)S(1)} all-to-all(bf16[16,1,64,128]{3,2,1,0:T(8,128)(2,1)S(1)} %broadcast_in_dim.191), channel_id=1, replica_groups=mesh['row'=16,'col'=16] {'col'}, dimensions={0} | all-to-all | bytes 524288 | tf_op jit(solution)/shard_map/all_to_all | solution.py:18
  282.5 10.1 %all-to-all-start.10 = ((bf16[16,256,256]{2,1,0:T(8,128)(2,1)}), bf16[16,256,256]{2,1,0:T(8,128)(2,1)S(1)}, u32[]{:S(2)}, u32[]{:S(2)}) async-start(bf16[16,256,256]{2,1,0:T(8,128)(2,1)} %stack.47), calls=%async_computation.10 | async-start | bytes 4194304 | tf_op jit(solution)/shard_map/all_to_all | solution.py:60
  295.6 48.0 %all-to-all-done.10 = bf16[16,256,256]{2,1,0:T(8,128)(2,1)S(1)} async-done(((bf16[16,256,256]{2,1,0:T(8,128)(2,1)}), bf16[16,256,256]{2,1,0:T(8,128)(2,1)S(1)}, u32[]{:S(2)}, u32[]{:S(2)}) %all-to-all-start.10) | async-done | bytes 2097184 | tf_op jit(solution)/shard_map/all_to_all | solution.py:60
  343.6 15.0 %all_to_all.93 = bf16[16,64,256]{2,1,0:T(8,128)(2,1)S(1)} all-to-all(bf16[16,64,256]{2,1,0:T(8,128)(2,1)S(1)} %broadcast_in_dim.195), channel_id=1, replica_groups=mesh['row'=16,'col'=16] {'col'}, dimensions={0} | all-to-all | bytes 1048576 | tf_op jit(solution)/shard_map/all_to_all | solution.py:18
  360.2 3.6 all-to-all-start.11
  364.4 9.1 %all-to-all-done.11 = bf16[16,64,256]{2,1,0:T(8,128)(2,1)S(1)} async-done(((bf16[16,64,256]{2,1,0:T(8,128)(2,1)}), bf16[16,64,256]{2,1,0:T(8,128)(2,1)S(1)}, u32[]{:S(2)}, u32[]{:S(2)}) %all-to-all-start.11) | async-done | bytes 524320 | tf_op jit(solution)/shard_map/all_to_all | solution.py:18
  373.6 2.4 fusion.6
  377.3 3.6 all-to-all-start.12
  382.2 10.4 %all-to-all-done.12 = bf16[16,3,64,128]{3,2,1,0:T(8,128)(2,1)S(1)} async-done(((bf16[16,3,64,128]{3,2,1,0:T(8,128)(2,1)}), bf16[16,3,64,128]{3,2,1,0:T(8,128)(2,1)S(1)}, u32[]{:S(2)}, u32[]{:S(2)}) %all-to-all-start.12) | async-done | bytes 786464 | tf_op jit(solution)/shard_map/all_to_all | solution.py:18
  393.8 3.6 all-to-all-start.13
  398.6 7.9 %all-to-all-done.13 = bf16[16,64,256]{2,1,0:T(8,128)(2,1)S(1)} async-done(((bf16[16,64,256]{2,1,0:T(8,128)(2,1)}), bf16[16,64,256]{2,1,0:T(8,128)(2,1)S(1)}, u32[]{:S(2)}, u32[]{:S(2)}) %all-to-all-start.13) | async-done | bytes 524320 | tf_op jit(solution)/shard_map/all_to_all | solution.py:18
  410.0 3.6 all-to-all-start.14
  414.9 7.7 %all-to-all-done.14 = bf16[16,2,64,128]{3,2,1,0:T(8,128)(2,1)S(1)} async-done(((bf16[16,2,64,128]{3,2,1,0:T(8,128)(2,1)}), bf16[16,2,64,128]{3,2,1,0:T(8,128)(2,1)S(1)}, u32[]{:S(2)}, u32[]{:S(2)}) %all-to-all-start.14) | async-done | bytes 524320 | tf_op jit(solution)/shard_map/all_to_all | solution.py:18
  422.9 11.6 %all_to_all.94 = bf16[16,64,256]{2,1,0:T(8,128)(2,1)S(1)} all-to-all(bf16[16,64,256]{2,1,0:T(8,128)(2,1)S(1)} %broadcast_in_dim.208), channel_id=1, replica_groups=mesh['row'=16,'col'=16] {'col'}, dimensions={0} | all-to-all | bytes 1048576 | tf_op jit(solution)/shard_map/all_to_all | solution.py:18
  434.6 2.4 fusion.2
  437.9 3.5 all-to-all-start.16
  441.5 7.5 %all-to-all-done.16 = bf16[16,1,64,128]{3,2,1,0:T(8,128)(2,1)S(1)} async-done(((bf16[16,1,64,128]{3,2,1,0:T(8,128)(2,1)}), bf16[16,1,64,128]{3,2,1,0:T(8,128)(2,1)S(1)}, u32[]{:S(2)}, u32[]{:S(2)}) %all-to-all-start.16) | async-done | bytes 262176 | tf_op jit(solution)/shard_map/all_to_all | solution.py:18
  449.2 11.6 %all_to_all.95 = bf16[16,64,256]{2,1,0:T(8,128)(2,1)S(1)} all-to-all(bf16[16,64,256]{2,1,0:T(8,128)(2,1)S(1)} %broadcast_in_dim.214), channel_id=1, replica_groups=mesh['row'=16,'col'=16] {'col'}, dimensions={0} | all-to-all | bytes 1048576 | tf_op jit(solution)/shard_map/all_to_all | solution.py:18
  (109 shorter events, 45.6 us)
Async XLA Ops:
  8.2 18.1 %all-to-all-start = ((bf16[16,64,256]{2,1,0:T(8,128)(2,1)}), bf16[16,64,256]{2,1,0:T(8,128)(2,1)S(1)}, u32[]{:S(2)}, u32[]{:S(2)}) async-start(bf16[16,64,256]{2,1,0:T(8,128)(2,1)} %broadcast_in_dim.83), calls=%async_computation | async-start | bytes 1048576 | tf_op jit(solution)/shard_map/all_to_all | solution.py:18
  27.9 10.6 %copy-start.7 = (s32[3]{0:T(128)S(1)}, s32[3]{0:T(128)}, u32[]{:S(2)}) copy-start(s32[3]{0:T(128)} %constant.313) | copy-start | bytes 40
  27.9 59.5 %all-to-all-start.1 = ((bf16[16,256,256]{2,1,0:T(8,128)(2,1)}), bf16[16,256,256]{2,1,0:T(8,128)(2,1)S(1)}, u32[]{:S(2)}, u32[]{:S(2)}) async-start(bf16[16,256,256]{2,1,0:T(8,128)(2,1)} %stack.40), calls=%async_computation.1 | async-start | bytes 4194304 | tf_op jit(solution)/shard_map/all_to_all | solution.py:60
  106.6 7.7 %copy-start = (s32[6]{0:T(128)S(1)}, s32[6]{0:T(128)}, u32[]{:S(2)}) copy-start(s32[6]{0:T(128)} %param.50) | copy-start | bytes 76
  106.6 55.1 %all-to-all-start.4 = ((bf16[16,256,256]{2,1,0:T(8,128)(2,1)}), bf16[16,256,256]{2,1,0:T(8,128)(2,1)S(1)}, u32[]{:S(2)}, u32[]{:S(2)}) async-start(bf16[16,256,256]{2,1,0:T(8,128)(2,1)} %stack.42), calls=%async_computation.4 | async-start | bytes 4194304 | tf_op jit(solution)/shard_map/all_to_all | solution.py:60
  112.8 53.4 %copy-start.6 = (s32[2]{0:T(128)S(1)}, s32[2]{0:T(128)}, u32[]{:S(2)}) copy-start(s32[2]{0:T(128)} %constant.316) | copy-start | bytes 28
  162.6 14.6 %all-to-all-start.3 = ((bf16[16,64,256]{2,1,0:T(8,128)(2,1)}), bf16[16,64,256]{2,1,0:T(8,128)(2,1)S(1)}, u32[]{:S(2)}, u32[]{:S(2)}) async-start(bf16[16,64,256]{2,1,0:T(8,128)(2,1)} %broadcast_in_dim.89), calls=%async_computation.3 | async-start | bytes 1048576 | tf_op jit(solution)/shard_map/all_to_all | solution.py:18
  193.1 61.2 %all-to-all-start.7 = ((bf16[16,256,256]{2,1,0:T(8,128)(2,1)}), bf16[16,256,256]{2,1,0:T(8,128)(2,1)S(1)}, u32[]{:S(2)}, u32[]{:S(2)}) async-start(bf16[16,256,256]{2,1,0:T(8,128)(2,1)} %stack.44), calls=%async_computation.7 | async-start | bytes 4194304 | tf_op jit(solution)/shard_map/all_to_all | solution.py:60
  199.8 173.8 %all-gather.9.cloned.1.call-start = ((), (), s32[]{:S(2)}) async-start(), calls=%async_computation.18 | async-start | bytes 2228224 | tf_op jit(solution)/shard_map/all_gather | solution.py:89
  255.1 13.5 %all-to-all-start.6 = ((bf16[16,64,256]{2,1,0:T(8,128)(2,1)}), bf16[16,64,256]{2,1,0:T(8,128)(2,1)S(1)}, u32[]{:S(2)}, u32[]{:S(2)}) async-start(bf16[16,64,256]{2,1,0:T(8,128)(2,1)} %broadcast_in_dim.187), calls=%async_computation.6 | async-start | bytes 1048576 | tf_op jit(solution)/shard_map/all_to_all | solution.py:18
  258.7 147.8 %all-gather.11.cloned.1.call-start = ((), (), s32[]{:S(2)}) async-start(), calls=%async_computation.19 | async-start | bytes 2228224 | tf_op jit(solution)/shard_map/all_gather | solution.py:89
  282.5 61.1 %all-to-all-start.10 = ((bf16[16,256,256]{2,1,0:T(8,128)(2,1)}), bf16[16,256,256]{2,1,0:T(8,128)(2,1)S(1)}, u32[]{:S(2)}, u32[]{:S(2)}) async-start(bf16[16,256,256]{2,1,0:T(8,128)(2,1)} %stack.47), calls=%async_computation.10 | async-start | bytes 4194304 | tf_op jit(solution)/shard_map/all_to_all | solution.py:60
  292.6 142.0 %all-gather.13.cloned.1.call-start = ((), (), s32[]{:S(2)}) async-start(), calls=%async_computation.20 | async-start | bytes 2228224 | tf_op jit(solution)/shard_map/all_gather | solution.py:89
  358.6 5.2 %copy-start.5 = (s32[3]{0:T(128)S(1)}, s32[3]{0:T(128)}, u32[]{:S(2)}) copy-start(s32[3]{0:T(128)} %constant.319) | copy-start | bytes 40
  358.6 5.2 %copy-start.2 = (bf16[6,256,128]{2,1,0:T(8,128)(2,1)S(1)}, bf16[6,256,128]{2,1,0:T(8,128)(2,1)}, u32[]{:S(2)}) copy-start(bf16[6,256,128]{2,1,0:T(8,128)(2,1)} %param.49) | copy-start | bytes 1179652
  360.2 13.3 %all-to-all-start.11 = ((bf16[16,64,256]{2,1,0:T(8,128)(2,1)}), bf16[16,64,256]{2,1,0:T(8,128)(2,1)S(1)}, u32[]{:S(2)}, u32[]{:S(2)}) async-start(bf16[16,64,256]{2,1,0:T(8,128)(2,1)} %broadcast_in_dim.196), calls=%async_computation.11 | async-start | bytes 1048576 | tf_op jit(solution)/shard_map/all_to_all | solution.py:18
  373.6 7.3 %copy-start.3 = (bf16[6,256,128]{2,1,0:T(8,128)(2,1)S(1)}, bf16[6,256,128]{2,1,0:T(8,128)(2,1)}, u32[]{:S(2)}) copy-start(bf16[6,256,128]{2,1,0:T(8,128)(2,1)} %param.48) | copy-start | bytes 1179652
  376.0 5.5 %copy-start.1 = (s32[6]{0:T(128)S(1)}, s32[6]{0:T(128)}, u32[]{:S(2)}) copy-start(s32[6]{0:T(128)} %param.51) | copy-start | bytes 76
  377.3 15.3 %all-to-all-start.12 = ((bf16[16,3,64,128]{3,2,1,0:T(8,128)(2,1)}), bf16[16,3,64,128]{3,2,1,0:T(8,128)(2,1)S(1)}, u32[]{:S(2)}, u32[]{:S(2)}) async-start(bf16[16,3,64,128]{3,2,1,0:T(8,128)(2,1)} %broadcast_in_dim.197), calls=%async_computation.12 | async-start | bytes 1572864 | tf_op jit(solution)/shard_map/all_to_all | solution.py:18
  380.9 17.1 %copy-start.4 = (s32[2]{0:T(128)S(1)}, s32[2]{0:T(128)}, u32[]{:S(2)}) copy-start(s32[2]{0:T(128)} %constant.322) | copy-start | bytes 28
  393.8 12.7 %all-to-all-start.13 = ((bf16[16,64,256]{2,1,0:T(8,128)(2,1)}), bf16[16,64,256]{2,1,0:T(8,128)(2,1)S(1)}, u32[]{:S(2)}, u32[]{:S(2)}) async-start(bf16[16,64,256]{2,1,0:T(8,128)(2,1)} %broadcast_in_dim.202), calls=%async_computation.13 | async-start | bytes 1048576 | tf_op jit(solution)/shard_map/all_to_all | solution.py:18
  397.4 63.5 %all-gather.15.cloned.1.call-start = ((), (), s32[]{:S(2)}) async-start(), calls=%async_computation.21 | async-start | bytes 2228224 | tf_op jit(solution)/shard_map/all_gather | solution.py:89
  410.0 12.5 %all-to-all-start.14 = ((bf16[16,2,64,128]{3,2,1,0:T(8,128)(2,1)}), bf16[16,2,64,128]{3,2,1,0:T(8,128)(2,1)S(1)}, u32[]{:S(2)}, u32[]{:S(2)}) async-start(bf16[16,2,64,128]{3,2,1,0:T(8,128)(2,1)} %broadcast_in_dim.203), calls=%async_computation.14 | async-start | bytes 1048576 | tf_op jit(solution)/shard_map/all_to_all | solution.py:18
  437.9 11.0 %all-to-all-start.16 = ((bf16[16,1,64,128]{3,2,1,0:T(8,128)(2,1)}), bf16[16,1,64,128]{3,2,1,0:T(8,128)(2,1)S(1)}, u32[]{:S(2)}, u32[]{:S(2)}) async-start(bf16[16,1,64,128]{3,2,1,0:T(8,128)(2,1)} %broadcast_in_dim.210), calls=%async_computation.16 | async-start | bytes 524288 | tf_op jit(solution)/shard_map/all_to_all | solution.py:18
Sparse Core Ops, SparseCore 0:
  202.3 62.9 all-gather.8
  267.1 54.5 all-gather.10
  323.5 49.5 all-gather.12
  399.7 43.4 all-gather.14
